TPU v7x, 128 devices: a whole 4x4x4 slice. The times are simulated.
128 devices in a mesh: leaf: 128 (over x, y, z, core).
Axes of the slice: x: 4, y: 4, z: 4, core: 2. Of those that a mesh axis runs over, the one named last changes fastest.
Arguments:
- weights: float32 [524288, 128], P('leaf'), may hold values from -6 to 6
- labels: int32 [524288], P('leaf'), may hold values from 0 to 127
- basis: bfloat16 [2048, 64, 256], P('leaf'), may hold values from -0.375 to 0.375
- near_tiles: bfloat16 [2048, 3, 256, 256], P('leaf'), may hold values from -0.21875 to 0.21875
- near_ids: int32 [2048, 2], P('leaf'), may hold values from 0 to 2047, as said below
- transfer: bfloat16 [3968, 64, 64], P('leaf'), may hold values from -0.5 to 0.5
- couplings: bfloat16 [3968, 64, 256], P('leaf'), may hold values from -0.375 to 0.375
- sources: int32 [3968, 4], P('leaf'), may hold values from 0 to 2047, as said below
- coarse_transfer: bfloat16 [124, 64, 64], replicated, may hold values from -0.5 to 0.5
- coarse_couplings: bfloat16 [126, 64, 256], replicated, may hold values from -0.375 to 0.375
- coarse_sources: int32 [126, 4], replicated, may hold values from 0 to 63, as said below
Outputs:
- updated: float32 [524288, 128], P('leaf')
- second_scores: float32 [524288, 128], P('leaf')
Inputs may be any that keep to these rules, and one draw needn't show every extreme that they name: `sources`: rows of device q's block name nodes of their row's level, numbered over all devices; the rows of one device name at most 1 nodes held by any single device (counted over all its rows), and some pair of devices reaches 1. `coarse_sources`: entries of a row name a node of that row's coarse level. `near_ids`: each entry lies within 2 leaves of its own leaf and differs from it; distance 2 occurs.
All inputs are finite; a program needn't handle non-finite values.
Results may differ from a plain program's by a relative error of at most 0.025.
Values may be sent and summed in bfloat16 or wider, within the bound.
A program may use at most 128 MiB of HBM per device.

v0:
```python
import functools

import jax
import jax.numpy as jnp
from jax import lax
from jax.experimental import pallas as pl
from jax.experimental.pallas import tpu as pltpu
from jax.sharding import PartitionSpec as P

MESH = pl.DeviceIdType.MESH
DEV = 128
LEAVES = 16
LEAF = 256
RANK = 64
NODES = 31
COLS = 128
HALO = 2
COARSE = 126
STARTS = (0, 16, 24, 28, 30)
COARSE_AT = (0, 64, 96, 112, 120, 124)
BATCH = 8
WINDOW = 4
STEP = 37


def mm(a, b):
    return jnp.dot(a, b, preferred_element_type=jnp.float32)


def within(i, count):
    return lax.max(lax.min(i, count - 1), 0)


def coords(me):
    return (
        lax.div(me, 32),
        lax.rem(lax.div(me, 8), 4),
        lax.rem(lax.div(me, 2), 4),
        lax.rem(me, 2),
    )


def partner_at(me, k):
    x, y, z, c = coords(me)
    dx, dy, dz, dc = coords(lax.rem(k * STEP, DEV))
    line = lax.rem(x + dx, 4) * 4 + lax.rem(y + dy, 4)
    return (line * 4 + lax.rem(z + dz, 4)) * 2 + lax.rem(c + dc, 2)


def remote(src, dst, send_sem, recv_sem, device):
    return pltpu.make_async_remote_copy(
        src_ref=src,
        dst_ref=dst,
        send_sem=send_sem,
        recv_sem=recv_sem,
        device_id=(device,),
        device_id_type=MESH,
    )


def take(ref, sem):
    pltpu.make_async_copy(ref, ref, sem).wait()


def kernel(
    sources_s,
    near_ids_s,
    coarse_sources_s,
    sources_v,
    labels_v,
    weights_h,
    basis_h,
    near_h,
    transfer_h,
    couplings_h,
    coarse_transfer_h,
    coarse_couplings_h,
    updated_h,
    scores_h,
    w,
    shift,
    vals0,
    vals1,
    acc,
    near,
    basis,
    basis_t,
    maps,
    maps_t,
    blocks,
    coef,
    field,
    coupled,
    send,
    recv0,
    recv1,
    request,
    requests,
    chosen_v,
    chosen,
    mate_map,
    mate_coef,
    own_coarse,
    coarse0,
    coarse1,
    planes_in,
    planes,
    cmaps,
    cmaps_t,
    cblocks,
    f1_out,
    f1_in,
    in_sem,
    coarse_sem,
    list_sem,
    halo_send,
    halo_recv,
    mate_sem,
    gather_send,
    gather_recv,
    block_send,
    block_recv,
    f1_send,
    f1_recv,
    small_sem,
    out_sem,
):
    me = lax.axis_index("leaf")
    vals, recv, coarse = (vals0, vals1), (recv0, recv1), (coarse0, coarse1)
    x, y, z, c = coords(me)
    line = x * 4 + y
    mate = me + 1 - 2 * c
    is_server = (z == lax.rem(x + y, 4)) & (c == 1 - lax.rem(y, 2))

    barrier = pltpu.get_barrier_semaphore()

    def greet(k, carry):
        pl.semaphore_signal(
            barrier, inc=1, device_id=(partner_at(me, k),), device_id_type=MESH
        )
        return carry

    lax.fori_loop(1, DEV, greet, 0)

    loads = [
        pltpu.make_async_copy(src, dst, in_sem.at[i])
        for i, (src, dst) in enumerate(
            (
                (weights_h, w),
                (basis_h, basis),
                (transfer_h, maps),
                (couplings_h, blocks),
                (near_h, near),
            )
        )
    ]
    for load in loads:
        load.start()

    coarse_rows = (
        (0, 4 * line, 4),
        (4, 64 + 2 * line, 2),
        (6, 96 + line, 1),
        (7, 112 + lax.div(line, 2), 1),
        (8, 120 + lax.div(line, 4), 1),
        (9, 124 + lax.div(line, 8), 1),
    )
    coarse_loads = [
        pltpu.make_async_copy(coarse_transfer_h, planes_in, coarse_sem.at[6])
    ] + [
        pltpu.make_async_copy(
            coarse_couplings_h.at[pl.ds(row, count)],
            cblocks.at[pl.ds(at, count)],
            coarse_sem.at[i],
        )
        for i, (at, row, count) in enumerate(coarse_rows)
    ]

    @pl.when(is_server)
    def _():
        for load in coarse_loads:
            load.start()

    node = lax.broadcasted_iota(jnp.int32, (4, NODES), 1)
    bits = jnp.full((4, NODES), 4, jnp.int32)
    first = jnp.zeros((4, NODES), jnp.int32)
    for height in range(1, 5):
        bits = jnp.where(node >= STARTS[height], 4 - height, bits)
        first = jnp.where(node >= STARTS[height], STARTS[height], first)
    name = sources_v[...]
    owner = lax.shift_right_logical(name, bits)
    row = first + name - lax.shift_left(owner, bits)
    pad = jnp.zeros((4, COLS - NODES), jnp.int32)
    owner = jnp.concatenate([owner, pad], axis=1).astype(jnp.float32)
    row = jnp.concatenate([row, pad], axis=1).astype(jnp.float32)
    device = lax.broadcasted_iota(jnp.int32, (COLS, COLS), 0)
    hits = jnp.zeros((8, COLS), jnp.float32)
    for k in range(4):
        at = jnp.broadcast_to(owner[k : k + 1], (COLS, COLS)).astype(jnp.int32)
        hot = (at == device).astype(jnp.float32).astype(jnp.bfloat16)
        rows = jnp.broadcast_to(row[k : k + 1], (8, COLS)).astype(jnp.bfloat16)
        hits += lax.dot_general(
            rows, hot, (((1,), (1,)), ((), ())), preferred_element_type=jnp.float32
        )
    asked = hits[0:1].astype(jnp.int32)
    request[...] = asked
    requests[pl.ds(me, 1)] = asked.reshape(1, 1, COLS)

    def half_round(t, carry):
        rows = pl.ds(pl.multiple_of(t * LEAF, LEAF), LEAF)
        v = w[rows, :].astype(jnp.bfloat16)
        vals0[t + HALO] = v
        coef[t] = mm(basis[t], v).astype(jnp.bfloat16)
        return carry

    def climb():
        for height in range(4):
            for j in range(LEAVES >> (height + 1)):
                lo = STARTS[height] + 2 * j
                up = STARTS[height + 1] + j
                kids = coef[lo : lo + 2].reshape(2 * RANK, COLS)
                coef[up] = mm(maps_t[up - LEAVES], kids).astype(jnp.bfloat16)

    loads[0].wait()
    loads[1].wait()
    lax.fori_loop(0, LEAVES, half_round, 0, unroll=4)
    loads[2].wait()

    def turn(j, carry):
        lo = 2 * j
        pair = maps[pl.ds(lo, 2)].reshape(2 * RANK, RANK)
        maps_t[j] = pair.astype(jnp.float32).T.astype(jnp.bfloat16)
        return carry

    lax.fori_loop(0, 15, turn, 0)
    climb()

    def turn_basis(t, carry):
        basis_t[t] = basis[t].astype(jnp.float32).T.astype(jnp.bfloat16)
        return carry

    lax.fori_loop(0, LEAVES, turn_basis, 0)

    lane = lax.broadcasted_iota(jnp.int32, (COLS, COLS), 1)

    def mark(i, carry):
        rows = pl.ds(pl.multiple_of(i * COLS, COLS), COLS)
        row = jnp.broadcast_to(labels_v[pl.ds(i, 1), :], (COLS, COLS))
        column = row.astype(jnp.float32).T.astype(jnp.int32)
        shift[rows, :] = jnp.where(column == lane, 0.25, -0.25).astype(jnp.bfloat16)
        return carry

    lax.fori_loop(0, LEAVES * LEAF // COLS, mark, 0)

    loads[3].wait()
    loads[4].wait()
    pl.semaphore_wait(barrier, DEV - 1)

    def halo_copies(phase):
        after = lax.rem(me + 1, DEV)
        before = lax.rem(me + DEV - 1, DEV)
        v = vals[phase]
        return (
            remote(
                v.at[pl.ds(LEAVES, HALO)],
                v.at[pl.ds(0, HALO)],
                halo_send.at[phase, 0],
                halo_recv.at[phase, 0],
                after,
            ),
            remote(
                v.at[pl.ds(HALO, HALO)],
                v.at[pl.ds(LEAVES + HALO, HALO)],
                halo_send.at[phase, 1],
                halo_recv.at[phase, 1],
                before,
            ),
        )

    def server_device(s):
        sx, sy = lax.div(s, 4), lax.rem(s, 4)
        sz = lax.rem(sx + sy, 4)
        return (s * 4 + sz) * 2 + 1 - lax.rem(sy, 2)

    def gather_copy(phase, i):
        return remote(
            own_coarse.at[phase],
            coarse[phase].at[lax.div(me, 2)],
            gather_send.at[phase],
            gather_recv.at[phase],
            server_device(2 * i + c),
        )

    def mate_copy(phase):
        return remote(
            coef.at[NODES - 1],
            mate_coef.at[phase],
            mate_sem.at[phase, 0],
            mate_sem.at[phase, 1],
            mate,
        )

    map_copy = remote(
        maps.at[NODES - 1], mate_map, mate_sem.at[2, 0], mate_sem.at[2, 1], mate
    )

    def list_copy(k):
        return remote(
            request,
            requests.at[me],
            list_sem.at[0],
            list_sem.at[1],
            partner_at(me, k),
        )

    def block_copy(phase, k, batch):
        to = partner_at(me, k)
        return remote(
            send.at[to],
            recv[phase].at[me],
            block_send.at[phase, batch],
            block_recv.at[phase],
            to,
        )

    def send_top(phase):
        mate_copy(phase).wait_recv()
        if phase == 0:
            map_copy.wait_recv()
            pair = jnp.concatenate(
                [
                    jnp.where(c == 0, maps[NODES - 1].astype(jnp.float32), mate_map[...].astype(jnp.float32)),
                    jnp.where(c == 0, mate_map[...].astype(jnp.float32), maps[NODES - 1].astype(jnp.float32)),
                ],
                axis=0,
            )
            maps_t[15] = pair.T.astype(jnp.bfloat16)
        mine = coef[NODES - 1].astype(jnp.float32)
        theirs = mate_coef[phase].astype(jnp.float32)
        kids = jnp.concatenate(
            [jnp.where(c == 0, mine, theirs), jnp.where(c == 0, theirs, mine)], axis=0
        ).astype(jnp.bfloat16)
        own_coarse[phase] = mm(maps_t[15], kids).astype(jnp.bfloat16)
        for i in range(8):
            gather_copy(phase, i).start()

    def fill(lo, hi):
        def one(d, carry):
            send[d] = coef[within(chosen[0, d], NODES)]
            return carry

        lax.fori_loop(lo, hi, one, 0, unroll=8)

    def near_leaf(phase, t):
        base = me * LEAVES - HALO
        a = within(near_ids_s[0, t] - base, LEAVES + 2 * HALO)
        b = within(near_ids_s[1, t] - base, LEAVES + 2 * HALO)
        rows = pl.ds(pl.multiple_of(t * LEAF, LEAF), LEAF)
        total = mm(near[t, 0], vals[phase][t + HALO])
        total += mm(near[t, 1], vals[phase][a])
        total += mm(near[t, 2], vals[phase][b])
        acc[rows, :] = total

    def send_batch(phase, batch):
        def one(i, carry):
            block_copy(phase, batch * BATCH + i, batch).start()
            return carry

        lax.fori_loop(jnp.where(batch == 0, 1, 0), BATCH, one, 0)

    def batch_sent(phase, batch, count=BATCH):
        take(send.at[pl.ds(0, count)], block_send.at[phase, batch])

    def serve(phase):
        table = coarse[phase]
        if phase == 0:
            for load in coarse_loads:
                load.wait()

            def flip(i, carry):
                plane = planes_in[i].astype(jnp.float32).T
                rows = pl.ds(pl.multiple_of(i * (COARSE - 2), 4), COARSE - 2)
                planes[rows, :] = plane
                return carry

            lax.fori_loop(0, RANK, flip, 0, unroll=4)

            def turn_coarse(j, carry):
                for n in (2 * j, 2 * j + 1):
                    one = planes[pl.ds(n, RANK, stride=COARSE - 2), :]
                    cmaps[n] = one.astype(jnp.bfloat16)
                pair = cmaps[pl.ds(2 * j, 2)].reshape(2 * RANK, RANK)
                cmaps_t[j] = pair.astype(jnp.float32).T.astype(jnp.bfloat16)
                return carry

            lax.fori_loop(0, 62, turn_coarse, 0, unroll=2)
        take(table.at[pl.ds(0, 64)], gather_recv.at[phase])
        for level in range(5):
            at, above = COARSE_AT[level], COARSE_AT[level + 1]

            def up(j, carry, at=at, above=above):
                lo = at + 2 * j
                kids = table[pl.ds(lo, 2)].reshape(2 * RANK, COLS)
                turned = cmaps_t[lax.div(lo, 2)]
                table[above + j] = mm(turned, kids).astype(jnp.bfloat16)
                return carry

            count = 32 >> level
            lax.fori_loop(0, count, up, 0, unroll=min(count, 4))

        def term(slot, level, row):
            at = COARSE_AT[level]
            kids = jnp.concatenate(
                [table[at + within(coarse_sources_s[k, row], DEV >> (level + 1))] for k in range(4)], axis=0
            )
            return mm(cblocks[slot], kids)

        rows = [row for _, row, _ in coarse_rows]
        terms = [
            term(slot, level, rows[level] + i)
            for level, (at, _, count) in enumerate(coarse_rows)
            for i, slot in enumerate(range(at, at + count))
        ]
        f = terms[9].astype(jnp.bfloat16)
        for slot, level in ((8, 4), (7, 3), (6, 2)):
            f = (terms[slot] + mm(cmaps[rows[level]], f)).astype(jnp.bfloat16)
        for i in range(2):
            g = (terms[4 + i] + mm(cmaps[rows[1] + i], f)).astype(jnp.bfloat16)
            for j in range(2):
                n = 2 * i + j
                f1_out[phase, n] = (
                    terms[n] + mm(cmaps[rows[0] + n], g)
                ).astype(jnp.bfloat16)
        for o in range(1, 8):
            f1_copy(phase, o).start()
        f1_in[phase] = f1_out[phase, z]

    def f1_copy(phase, o):
        tz = lax.rem(z + o // 2, 4)
        to = (line * 4 + tz) * 2 + lax.rem(c + o % 2, 2)
        return remote(
            f1_out.at[phase, tz],
            f1_in.at[phase],
            f1_send.at[phase],
            f1_recv.at[phase],
            to,
        )

    def exchange(phase):
        for batch in range(WINDOW):
            send_batch(phase, batch)
        for h in halo_copies(phase):
            h.wait_recv()

        def step(t, carry):
            near_leaf(phase, t)
            near_leaf(phase, t + 1)
            for i in range(2):
                batch = t + i + WINDOW

                @pl.when(batch < DEV // BATCH)
                def _():
                    send_batch(phase, batch)

            return carry

        def pair(i, carry):
            return step(2 * i, carry)

        lax.fori_loop(0, 2, pair, 0)

        @pl.when(is_server)
        def _():
            serve(phase)

        lax.fori_loop(2, LEAVES // 2, pair, 0)

    def finish(phase):
        take(recv[phase].at[pl.ds(0, DEV - 1)], block_recv.at[phase])

        def couple(t, bits):
            kids = jnp.concatenate(
                [
                    recv[phase][within(lax.shift_right_logical(sources_s[k, t], bits), DEV)]
                    for k in range(4)
                ],
                axis=0,
            )
            coupled[t] = mm(blocks[t], kids)

        def leaf_pair(t, carry):
            couple(t, 4)
            return carry

        for t in range(NODES - 1, LEAVES - 1, -1):
            height = max(h for h in range(5) if t >= STARTS[h])
            couple(t, 4 - height)
        lax.fori_loop(0, LEAVES, leaf_pair, 0, unroll=4)

        @pl.when(jnp.logical_not(is_server))
        def _():
            take(f1_in.at[phase], f1_recv.at[phase])

        field[NODES - 1] = (
            coupled[NODES - 1] + mm(maps[NODES - 1], f1_in[phase])
        ).astype(jnp.bfloat16)
        for height in range(3, -1, -1):
            for j in range(LEAVES >> (height + 1)):
                lo = STARTS[height] + 2 * j
                pushed = mm(
                    maps[lo : lo + 2].reshape(2 * RANK, RANK),
                    field[STARTS[height + 1] + j],
                )
                both = coupled[lo : lo + 2] + pushed.reshape(2, RANK, COLS)
                field[lo : lo + 2] = both.astype(jnp.bfloat16)

    def first_leaf(t, carry):
        rows = pl.ds(pl.multiple_of(t * LEAF, LEAF), LEAF)
        score = acc[rows, :] + mm(basis_t[t], field[t])
        moved = shift[rows, :].astype(jnp.float32) - 0.25 * jnp.tanh(0.5 * score)
        middle = w[rows, :] + moved
        w[rows, :] = middle
        v = middle.astype(jnp.bfloat16)
        vals1[t + HALO] = v
        coef[t] = mm(basis[t], v).astype(jnp.bfloat16)
        return carry

    def last_leaf(t, carry):
        rows = pl.ds(pl.multiple_of(t * LEAF, LEAF), LEAF)
        score = acc[rows, :] + mm(basis_t[t], field[t])
        acc[rows, :] = score
        moved = shift[rows, :].astype(jnp.float32) - 0.25 * jnp.tanh(0.5 * score)
        w[rows, :] = w[rows, :] + moved
        return carry

    map_copy.start()
    mate_copy(0).start()

    def ask(k, carry):
        list_copy(k).start()
        return carry

    lax.fori_loop(1, DEV, ask, 0)
    for h in halo_copies(0):
        h.start()
    send_top(0)

    take(requests.at[pl.ds(0, DEV - 1)], list_sem.at[1])
    mine = (lax.broadcasted_iota(jnp.int32, (8, DEV), 1) == me).astype(jnp.bfloat16)
    table = requests[...].reshape(DEV, COLS).astype(jnp.float32).astype(jnp.bfloat16)
    wanted = lax.dot_general(
        mine, table, (((1,), (1,)), ((), ())), preferred_element_type=jnp.float32
    )
    chosen_v[...] = jnp.clip(wanted, 0, NODES - 1).astype(jnp.int32)
    small = pltpu.make_async_copy(chosen_v, chosen, small_sem)
    small.start()
    small.wait()

    fill(0, DEV)
    recv0[me] = coef[within(chosen[0, me], NODES)]
    exchange(0)
    finish(0)
    lax.fori_loop(0, LEAVES, first_leaf, 0, unroll=2)

    for batch in range(DEV // BATCH):
        batch_sent(0, batch, BATCH - 1 if batch == 0 else BATCH)
    mate_copy(0).wait_send()
    for h in halo_copies(1):
        h.start()
    climb()
    mate_copy(1).start()
    fill(0, DEV)
    recv1[me] = coef[within(chosen[0, me], NODES)]
    send_top(1)
    exchange(1)
    finish(1)
    lax.fori_loop(0, LEAVES, last_leaf, 0, unroll=2)
    outs = [
        pltpu.make_async_copy(w, updated_h, out_sem.at[0]),
        pltpu.make_async_copy(acc, scores_h, out_sem.at[1]),
    ]
    for out in outs:
        out.start()

    map_copy.wait_send()
    take(requests.at[pl.ds(0, DEV - 1)], list_sem.at[0])
    mate_copy(1).wait_send()
    for batch in range(DEV // BATCH):
        batch_sent(1, batch, BATCH - 1 if batch == 0 else BATCH)
    for phase in range(2):
        for h in halo_copies(phase):
            h.wait_send()
        take(coarse[phase].at[pl.ds(0, 8)], gather_send.at[phase])

        @pl.when(is_server)
        def _():
            take(coarse[phase].at[pl.ds(0, 7)], f1_send.at[phase])

    for out in outs:
        out.wait()


def local(
    weights,
    labels,
    basis,
    near_tiles,
    near_ids,
    transfer,
    couplings,
    sources,
    coarse_transfer,
    coarse_couplings,
    coarse_sources,
):
    bf16, f32, i32 = jnp.bfloat16, jnp.float32, jnp.int32
    points = LEAVES * LEAF
    smem = pl.BlockSpec(memory_space=pltpu.SMEM)
    vmem = pl.BlockSpec(memory_space=pltpu.VMEM)
    hbm = pl.BlockSpec(memory_space=pl.ANY)
    dma = pltpu.SemaphoreType.DMA
    scratch = [
        pltpu.VMEM((points, COLS), f32),
        pltpu.VMEM((points, COLS), bf16),
        pltpu.VMEM((LEAVES + 2 * HALO, LEAF, COLS), bf16),
        pltpu.VMEM((LEAVES + 2 * HALO, LEAF, COLS), bf16),
        pltpu.VMEM((points, COLS), f32),
        pltpu.VMEM((LEAVES, 3, LEAF, LEAF), bf16),
        pltpu.VMEM((LEAVES, RANK, LEAF), bf16),
        pltpu.VMEM((LEAVES, LEAF, RANK), bf16),
        pltpu.VMEM((NODES, RANK, RANK), bf16),
        pltpu.VMEM((16, RANK, 2 * RANK), bf16),
        pltpu.VMEM((NODES, RANK, 4 * RANK), bf16),
        pltpu.VMEM((NODES, RANK, COLS), bf16),
        pltpu.VMEM((NODES, RANK, COLS), bf16),
        pltpu.VMEM((NODES, RANK, COLS), f32),
        pltpu.VMEM((DEV, RANK, COLS), bf16),
        pltpu.VMEM((DEV, RANK, COLS), bf16),
        pltpu.VMEM((DEV, RANK, COLS), bf16),
        pltpu.VMEM((1, COLS), i32),
        pltpu.VMEM((DEV, 1, COLS), i32),
        pltpu.VMEM((8, DEV), i32),
        pltpu.SMEM((8, DEV), i32),
        pltpu.VMEM((RANK, RANK), bf16),
        pltpu.VMEM((2, RANK, COLS), bf16),
        pltpu.VMEM((2, RANK, COLS), bf16),
        pltpu.VMEM((COARSE, RANK, COLS), bf16),
        pltpu.VMEM((COARSE, RANK, COLS), bf16),
        pltpu.VMEM((RANK, RANK, COARSE - 2), bf16),
        pltpu.VMEM(((RANK + 1) * (COARSE - 2), RANK), f32),
        pltpu.VMEM((COARSE - 2, RANK, RANK), bf16),
        pltpu.VMEM((62, RANK, 2 * RANK), bf16),
        pltpu.VMEM((10, RANK, 4 * RANK), bf16),
        pltpu.VMEM((2, 4, RANK, COLS), bf16),
        pltpu.VMEM((2, RANK, COLS), bf16),
        dma((5,)),
        dma((7,)),
        dma((2,)),
        dma((2, 2)),
        dma((2, 2)),
        dma((3, 2)),
        dma((2,)),
        dma((2,)),
        dma((2, DEV // BATCH)),
        dma((2,)),
        dma((2,)),
        dma((2,)),
        dma(()),
        dma((2,)),
    ]
    return pl.pallas_call(
        kernel,
        out_shape=(
            jax.ShapeDtypeStruct((points, COLS), f32),
            jax.ShapeDtypeStruct((points, COLS), f32),
        ),
        in_specs=[smem, smem, smem, vmem, vmem] + [hbm] * 7,
        out_specs=(hbm, hbm),
        scratch_shapes=scratch,
        compiler_params=pltpu.CompilerParams(
            collective_id=0, has_side_effects=True, vmem_limit_bytes=58 << 20
        ),
    )(
        sources.T,
        near_ids.T,
        coarse_sources.T,
        sources.T,
        labels.reshape(points // COLS, COLS),
        weights,
        basis,
        near_tiles,
        transfer,
        couplings,
        coarse_transfer.transpose(1, 2, 0),
        coarse_couplings,
    )


def solution(mesh):
    in_specs = (
        P("leaf", None),
        P("leaf"),
        P("leaf", None, None),
        P("leaf", None, None, None),
        P("leaf", None),
        P("leaf", None, None),
        P("leaf", None, None),
        P("leaf", None),
        P(),
        P(),
        P(),
    )
    out_specs = (P("leaf", None), P("leaf", None))
    return jax.shard_map(local, mesh=mesh, in_specs=in_specs, out_specs=out_specs, check_vma=False)
```

profile of v0, /device:TPU:1, one launch (start us, length us, event | category | flops | bytes accessed | tf_op | source)
XLA Modules:
  0.0 139.1 jit_solution(7139153613742509686)
XLA Ops:
  0.6 134.0 %shard_map.122 = (f32[4096,128]{1,0:T(8,128)}, f32[4096,128]{1,0:T(8,128)}) custom-call(s32[4,31]{1,0:T(4,128)} %bitcast.7, s32[2,16]{1,0:T(2,128)} %bitcast.10, s32[4,126]{1,0:T(4,128)} %bitcast.9, s32[4,31]{1,0:T(4,128)} %bitcast.8, s32[32,128]{1,0:T(8,128)} %bitcast.6, f32[4096,128]{1,0:T(8,128)} %weights_h.1, bf16[16,64,256]{2,1,0:T(8,128)(2,1)} %basis_h.1, ...), custom_call_target="tpu_custom_call" | custom-call | tf_op jit(solution)/shard_map/pallas_call | solution.py:671
  134.6 0.0 copy-start
  134.6 3.2 %copy.15 = f32[4096,128]{1,0:T(8,128)} copy(f32[4096,128]{1,0:T(8,128)} %get-tuple-element.4) | data formatting | bytes 4194304
  137.8 0.0 copy-done
  137.8 1.3 copy.16
Async XLA Ops:
  134.6 3.2 %copy-start = (f32[4096,128]{1,0:T(8,128)S(1)}, f32[4096,128]{1,0:T(8,128)}, u32[]{:S(2)}) copy-start(f32[4096,128]{1,0:T(8,128)} %get-tuple-element.5) | copy-start | bytes 6291460
where the time goes:
time: 139 us
  Pallas kernels  134 us (96%)
  local copies, waits for them, and re-layouts  4.52 us (3%)
    pallas_call x1, Pallas kernels, local(): pl.pallas_call(kernel, out_shape=(jax.ShapeDtypeStruct((points, COLS), f3...  134 us
    unnamed x4, local copies, waits for them, and re-layouts  4.52 us

commit v1 on v0

--- a/solution.py
+++ b/solution.py
@@ -19,8 +19,7 @@
 STARTS = (0, 16, 24, 28, 30)
 COARSE_AT = (0, 64, 96, 112, 120, 124)
 BATCH = 8
-WINDOW = 4
-STEP = 37
+BATCHES = DEV // BATCH
 
 
 def mm(a, b):
@@ -40,11 +39,28 @@
     )
 
 
-def partner_at(me, k):
+def batch_of(me, b):
     x, y, z, c = coords(me)
-    dx, dy, dz, dc = coords(lax.rem(k * STEP, DEV))
-    line = lax.rem(x + dx, 4) * 4 + lax.rem(y + dy, 4)
-    return (line * 4 + lax.rem(z + dz, 4)) * 2 + lax.rem(c + dc, 2)
+    bx, by = lax.div(b, 4), lax.rem(b, 4)
+    xs = [lax.rem(x + bx + j, 4) * 32 for j in range(4)]
+    ys = [lax.rem(y + by + j, 4) * 8 for j in range(4)]
+    zs = [lax.rem(z + j, 4) * 2 for j in range(4)]
+    cs = [c, 1 - c]
+    return [
+        xs[j] + ys[(j + 2 * k) % 4] + zs[j] + cs[k] for j in range(4) for k in range(2)
+    ]
+
+
+def for_all(me, act):
+    for device in batch_of(me, 0)[1:]:
+        act(device)
+
+    def one(b, carry):
+        for device in batch_of(me, b):
+            act(device)
+        return carry
+
+    lax.fori_loop(1, BATCHES, one, 0)
 
 
 def remote(src, dst, send_sem, recv_sem, device):
@@ -75,9 +91,10 @@
     couplings_h,
     coarse_transfer_h,
     coarse_couplings_h,
-    updated_h,
-    scores_h,
+    updated,
+    scores,
     w,
+    based,
     shift,
     vals0,
     vals1,
@@ -123,7 +140,6 @@
     f1_send,
     f1_recv,
     small_sem,
-    out_sem,
 ):
     me = lax.axis_index("leaf")
     vals, recv, coarse = (vals0, vals1), (recv0, recv1), (coarse0, coarse1)
@@ -134,13 +150,10 @@
 
     barrier = pltpu.get_barrier_semaphore()
 
-    def greet(k, carry):
+    def greet(device):
         pl.semaphore_signal(
-            barrier, inc=1, device_id=(partner_at(me, k),), device_id_type=MESH
+            barrier, inc=1, device_id=(device,), device_id_type=MESH
         )
-        return carry
-
-    lax.fori_loop(1, DEV, greet, 0)
 
     loads = [
         pltpu.make_async_copy(src, dst, in_sem.at[i])
@@ -156,6 +169,7 @@
     ]
     for load in loads:
         load.start()
+    for_all(me, greet)
 
     coarse_rows = (
         (0, 4 * line, 4),
@@ -232,14 +246,12 @@
         maps_t[j] = pair.astype(jnp.float32).T.astype(jnp.bfloat16)
         return carry
 
-    lax.fori_loop(0, 15, turn, 0)
+    lax.fori_loop(0, 15, turn, 0, unroll=5)
     climb()
 
     def turn_basis(t, carry):
         basis_t[t] = basis[t].astype(jnp.float32).T.astype(jnp.bfloat16)
         return carry
-
-    lax.fori_loop(0, LEAVES, turn_basis, 0)
 
     lane = lax.broadcasted_iota(jnp.int32, (COLS, COLS), 1)
 
@@ -250,10 +262,6 @@
         shift[rows, :] = jnp.where(column == lane, 0.25, -0.25).astype(jnp.bfloat16)
         return carry
 
-    lax.fori_loop(0, LEAVES * LEAF // COLS, mark, 0)
-
-    loads[3].wait()
-    loads[4].wait()
     pl.semaphore_wait(barrier, DEV - 1)
 
     def halo_copies(phase):
@@ -304,24 +312,19 @@
         maps.at[NODES - 1], mate_map, mate_sem.at[2, 0], mate_sem.at[2, 1], mate
     )
 
-    def list_copy(k):
-        return remote(
-            request,
-            requests.at[me],
-            list_sem.at[0],
-            list_sem.at[1],
-            partner_at(me, k),
-        )
-
-    def block_copy(phase, k, batch):
-        to = partner_at(me, k)
-        return remote(
-            send.at[to],
+    def list_copy(device):
+        remote(
+            request, requests.at[me], list_sem.at[0], list_sem.at[1], device
+        ).start()
+
+    def block_copy(phase, device):
+        remote(
+            send.at[device],
             recv[phase].at[me],
-            block_send.at[phase, batch],
+            block_send.at[phase],
             block_recv.at[phase],
-            to,
-        )
+            device,
+        ).start()
 
     def send_top(phase):
         mate_copy(phase).wait_recv()
@@ -361,52 +364,51 @@
         total += mm(near[t, 2], vals[phase][b])
         acc[rows, :] = total
 
-    def send_batch(phase, batch):
-        def one(i, carry):
-            block_copy(phase, batch * BATCH + i, batch).start()
+    def send_blocks(phase):
+        for_all(me, lambda device: block_copy(phase, device))
+
+    def blocks_sent(phase):
+        take(send.at[pl.ds(0, DEV - 1)], block_send.at[phase])
+
+    def prepare_server():
+        for load in coarse_loads:
+            load.wait()
+
+        def flip(i, carry):
+            plane = planes_in[i].astype(jnp.float32).T
+            rows = pl.ds(pl.multiple_of(i * (COARSE - 2), 4), COARSE - 2)
+            planes[rows, :] = plane
             return carry
 
-        lax.fori_loop(jnp.where(batch == 0, 1, 0), BATCH, one, 0)
-
-    def batch_sent(phase, batch, count=BATCH):
-        take(send.at[pl.ds(0, count)], block_send.at[phase, batch])
+        lax.fori_loop(0, RANK, flip, 0, unroll=4)
+
+        def turn_coarse(j, carry):
+            for n in (2 * j, 2 * j + 1):
+                one = planes[pl.ds(n, RANK, stride=COARSE - 2), :]
+                cmaps[n] = one.astype(jnp.bfloat16)
+            pair = cmaps[pl.ds(2 * j, 2)].reshape(2 * RANK, RANK)
+            cmaps_t[j] = pair.astype(jnp.float32).T.astype(jnp.bfloat16)
+            return carry
+
+        lax.fori_loop(0, 62, turn_coarse, 0, unroll=2)
 
     def serve(phase):
         table = coarse[phase]
-        if phase == 0:
-            for load in coarse_loads:
-                load.wait()
-
-            def flip(i, carry):
-                plane = planes_in[i].astype(jnp.float32).T
-                rows = pl.ds(pl.multiple_of(i * (COARSE - 2), 4), COARSE - 2)
-                planes[rows, :] = plane
-                return carry
-
-            lax.fori_loop(0, RANK, flip, 0, unroll=4)
-
-            def turn_coarse(j, carry):
-                for n in (2 * j, 2 * j + 1):
-                    one = planes[pl.ds(n, RANK, stride=COARSE - 2), :]
-                    cmaps[n] = one.astype(jnp.bfloat16)
-                pair = cmaps[pl.ds(2 * j, 2)].reshape(2 * RANK, RANK)
-                cmaps_t[j] = pair.astype(jnp.float32).T.astype(jnp.bfloat16)
-                return carry
-
-            lax.fori_loop(0, 62, turn_coarse, 0, unroll=2)
         take(table.at[pl.ds(0, 64)], gather_recv.at[phase])
         for level in range(5):
             at, above = COARSE_AT[level], COARSE_AT[level + 1]
 
-            def up(j, carry, at=at, above=above):
-                lo = at + 2 * j
-                kids = table[pl.ds(lo, 2)].reshape(2 * RANK, COLS)
-                turned = cmaps_t[lax.div(lo, 2)]
-                table[above + j] = mm(turned, kids).astype(jnp.bfloat16)
-                return carry
-
-            count = 32 >> level
-            lax.fori_loop(0, count, up, 0, unroll=min(count, 4))
+            group = min(32 >> level, 8)
+            for j in range(0, 32 >> level, group):
+                made = [
+                    mm(
+                        cmaps_t[at // 2 + i],
+                        table[at + 2 * i : at + 2 * i + 2].reshape(2 * RANK, COLS),
+                    ).astype(jnp.bfloat16)
+                    for i in range(j, j + group)
+                ]
+                for i in range(group):
+                    table[above + j + i] = made[i]
 
         def term(slot, level, row):
             at = COARSE_AT[level]
@@ -447,35 +449,29 @@
         )
 
     def exchange(phase):
-        for batch in range(WINDOW):
-            send_batch(phase, batch)
-        for h in halo_copies(phase):
-            h.wait_recv()
-
-        def step(t, carry):
-            near_leaf(phase, t)
-            near_leaf(phase, t + 1)
-            for i in range(2):
-                batch = t + i + WINDOW
-
-                @pl.when(batch < DEV // BATCH)
-                def _():
-                    send_batch(phase, batch)
-
-            return carry
-
-        def pair(i, carry):
-            return step(2 * i, carry)
-
-        lax.fori_loop(0, 2, pair, 0)
+        if phase == 0:
+            lax.fori_loop(0, LEAVES, turn_basis, 0, unroll=4)
+            lax.fori_loop(0, LEAVES * LEAF // COLS, mark, 0, unroll=4)
 
         @pl.when(is_server)
         def _():
             serve(phase)
 
-        lax.fori_loop(2, LEAVES // 2, pair, 0)
+        for h in halo_copies(phase):
+            h.wait_recv()
+        if phase == 0:
+            loads[4].wait()
+
+        def pair(t, carry):
+            near_leaf(phase, 2 * t)
+            near_leaf(phase, 2 * t + 1)
+            return carry
+
+        lax.fori_loop(0, LEAVES // 2, pair, 0)
 
     def finish(phase):
+        if phase == 0:
+            loads[3].wait()
         take(recv[phase].at[pl.ds(0, DEV - 1)], block_recv.at[phase])
 
         def couple(t, bits):
@@ -517,33 +513,32 @@
     def first_leaf(t, carry):
         rows = pl.ds(pl.multiple_of(t * LEAF, LEAF), LEAF)
         score = acc[rows, :] + mm(basis_t[t], field[t])
-        moved = shift[rows, :].astype(jnp.float32) - 0.25 * jnp.tanh(0.5 * score)
-        middle = w[rows, :] + moved
-        w[rows, :] = middle
+        marked = shift[rows, :].astype(jnp.float32)
+        middle = w[rows, :] + (marked - 0.25 * jnp.tanh(0.5 * score))
+        based[rows, :] = middle + marked
         v = middle.astype(jnp.bfloat16)
         vals1[t + HALO] = v
-        coef[t] = mm(basis[t], v).astype(jnp.bfloat16)
+        return carry
+
+    def second_coef(t, carry):
+        coef[t] = mm(basis[t], vals1[t + HALO]).astype(jnp.bfloat16)
         return carry
 
     def last_leaf(t, carry):
         rows = pl.ds(pl.multiple_of(t * LEAF, LEAF), LEAF)
         score = acc[rows, :] + mm(basis_t[t], field[t])
-        acc[rows, :] = score
-        moved = shift[rows, :].astype(jnp.float32) - 0.25 * jnp.tanh(0.5 * score)
-        w[rows, :] = w[rows, :] + moved
+        scores[rows, :] = score
+        updated[rows, :] = based[rows, :] - 0.25 * jnp.tanh(0.5 * score)
         return carry
 
     map_copy.start()
     mate_copy(0).start()
 
-    def ask(k, carry):
-        list_copy(k).start()
-        return carry
-
-    lax.fori_loop(1, DEV, ask, 0)
-    for h in halo_copies(0):
-        h.start()
-    send_top(0)
+    for_all(me, list_copy)
+
+    @pl.when(is_server)
+    def _():
+        prepare_server()
 
     take(requests.at[pl.ds(0, DEV - 1)], list_sem.at[1])
     mine = (lax.broadcasted_iota(jnp.int32, (8, DEV), 1) == me).astype(jnp.bfloat16)
@@ -554,39 +549,36 @@
     chosen_v[...] = jnp.clip(wanted, 0, NODES - 1).astype(jnp.int32)
     small = pltpu.make_async_copy(chosen_v, chosen, small_sem)
     small.start()
+    send_top(0)
+    for h in halo_copies(0):
+        h.start()
     small.wait()
-
     fill(0, DEV)
     recv0[me] = coef[within(chosen[0, me], NODES)]
+    send_blocks(0)
     exchange(0)
     finish(0)
-    lax.fori_loop(0, LEAVES, first_leaf, 0, unroll=2)
-
-    for batch in range(DEV // BATCH):
-        batch_sent(0, batch, BATCH - 1 if batch == 0 else BATCH)
-    mate_copy(0).wait_send()
+    lax.fori_loop(0, LEAVES, first_leaf, 0, unroll=4)
     for h in halo_copies(1):
         h.start()
+    lax.fori_loop(0, LEAVES, second_coef, 0, unroll=4)
+
+    blocks_sent(0)
+    mate_copy(0).wait_send()
     climb()
     mate_copy(1).start()
     fill(0, DEV)
     recv1[me] = coef[within(chosen[0, me], NODES)]
     send_top(1)
+    send_blocks(1)
     exchange(1)
     finish(1)
-    lax.fori_loop(0, LEAVES, last_leaf, 0, unroll=2)
-    outs = [
-        pltpu.make_async_copy(w, updated_h, out_sem.at[0]),
-        pltpu.make_async_copy(acc, scores_h, out_sem.at[1]),
-    ]
-    for out in outs:
-        out.start()
+    lax.fori_loop(0, LEAVES, last_leaf, 0, unroll=4)
 
     map_copy.wait_send()
     take(requests.at[pl.ds(0, DEV - 1)], list_sem.at[0])
     mate_copy(1).wait_send()
-    for batch in range(DEV // BATCH):
-        batch_sent(1, batch, BATCH - 1 if batch == 0 else BATCH)
+    blocks_sent(1)
     for phase in range(2):
         for h in halo_copies(phase):
             h.wait_send()
@@ -595,9 +587,6 @@
         @pl.when(is_server)
         def _():
             take(coarse[phase].at[pl.ds(0, 7)], f1_send.at[phase])
-
-    for out in outs:
-        out.wait()
 
 
 def local(
@@ -620,6 +609,7 @@
     hbm = pl.BlockSpec(memory_space=pl.ANY)
     dma = pltpu.SemaphoreType.DMA
     scratch = [
+        pltpu.VMEM((points, COLS), f32),
         pltpu.VMEM((points, COLS), f32),
         pltpu.VMEM((points, COLS), bf16),
         pltpu.VMEM((LEAVES + 2 * HALO, LEAF, COLS), bf16),
@@ -661,21 +651,20 @@
         dma((3, 2)),
         dma((2,)),
         dma((2,)),
-        dma((2, DEV // BATCH)),
+        dma((2,)),
         dma((2,)),
         dma((2,)),
         dma((2,)),
         dma(()),
-        dma((2,)),
     ]
     return pl.pallas_call(
         kernel,
         out_shape=(
-            jax.ShapeDtypeStruct((points, COLS), f32),
-            jax.ShapeDtypeStruct((points, COLS), f32),
+            pltpu.VMEM((points, COLS), f32),
+            pltpu.VMEM((points, COLS), f32),
         ),
         in_specs=[smem, smem, smem, vmem, vmem] + [hbm] * 7,
-        out_specs=(hbm, hbm),
+        out_specs=(vmem, vmem),
         scratch_shapes=scratch,
         compiler_params=pltpu.CompilerParams(
             collective_id=0, has_side_effects=True, vmem_limit_bytes=58 << 20

time: 139 us -> 94.8 us (0.68); the launches traced: 139 us -> 93.3 us
  Pallas kernels: 134 us -> 90 us
  local copies, waits for them, and re-layouts: 4.52 us -> 2.64 us
    pallas_call x1, Pallas kernels: 134 us -> 90 us  [local(): pl.pallas_call(kernel, out_shape=(pltpu.VMEM((points, COLS), f32), pltpu....]
    unnamed x4 -> x2, local copies, waits for them, and re-layouts: 4.52 us -> 2.64 us
where the time goes in v1:
time: 94.8 us; the launch traced here: 93.3 us
  Pallas kernels  90 us (95%)
  local copies, waits for them, and re-layouts  2.64 us (3%)
    pallas_call x1, Pallas kernels, local(): pl.pallas_call(kernel, out_shape=(pltpu.VMEM((points, COLS), f32), pltpu....  90 us
    unnamed x2, local copies, waits for them, and re-layouts  2.64 us

profile of v1, /device:TPU:1, one launch (start us, length us, event | category | flops | bytes accessed | tf_op | source)
XLA Modules:
  0.0 93.3 jit_solution(18174307154585580607)
XLA Ops:
  0.6 90.0 %shard_map.122 = (f32[4096,128]{1,0:T(8,128)S(1)}, f32[4096,128]{1,0:T(8,128)S(1)}) custom-call(s32[4,31]{1,0:T(4,128)} %bitcast.7, s32[2,16]{1,0:T(2,128)} %bitcast.10, s32[4,126]{1,0:T(4,128)} %bitcast.9, s32[4,31]{1,0:T(4,128)} %bitcast.8, s32[32,128]{1,0:T(8,128)} %bitcast.6, f32[4096,128]{1,0:T(8,128)} %weights_h.1, bf16[16,64,256]{2,1,0:T(8,128)(2,1)} %basis_h.1, ...), custom_call_target="tpu_custom_call" | custom-call | tf_op jit(solution)/shard_map/pallas_call | solution.py:660
  90.7 1.3 %copy.15 = f32[4096,128]{1,0:T(8,128)} copy(f32[4096,128]{1,0:T(8,128)S(1)} %get-tuple-element.2) | data formatting | bytes 4194304
  92.0 1.3 %copy.16 = f32[4096,128]{1,0:T(8,128)} copy(f32[4096,128]{1,0:T(8,128)S(1)} %get-tuple-element.3) | data formatting | bytes 4194304

commit v2 on v1

--- a/solution.py
+++ b/solution.py
@@ -26,6 +26,42 @@
     return jnp.dot(a, b, preferred_element_type=jnp.float32)
 
 
+def pack(wide, turn):
+    group = lax.div(lax.broadcasted_iota(jnp.int32, (16, COLS), 1), 32)
+    out = wide[0:16]
+    if turn % 4:
+        out = pltpu.roll(out, 32 * (turn % 4), 1)
+    for g in range(1, 4):
+        part = wide[16 * g : 16 * g + 16]
+        by = (g + turn) % 4
+        if by:
+            part = pltpu.roll(part, 32 * by, 1)
+        out = jnp.where(group == g, part, out)
+    return out.astype(jnp.bfloat16)
+
+
+def unpack(ref, node):
+    part = ref[node].astype(jnp.float32)
+    parts = [part] + [pltpu.roll(part, 32 * (4 - g), 1) for g in range(1, 4)]
+    return jnp.concatenate(parts, axis=0).astype(jnp.bfloat16)
+
+
+def join(ref, phase):
+    group = lax.div(lax.broadcasted_iota(jnp.int32, (16, COLS), 1), 32)
+    parts = [ref[phase, v].astype(jnp.float32) for v in range(4)]
+    rows = []
+    for g in range(4):
+        row = parts[0]
+        if g:
+            row = pltpu.roll(row, 32 * (4 - g), 1)
+        for v in range(1, 4):
+            by = (v - g) % 4
+            part = pltpu.roll(parts[v], 32 * by, 1) if by else parts[v]
+            row = jnp.where(group == v, part, row)
+        rows.append(row)
+    return jnp.concatenate(rows, axis=0).astype(jnp.bfloat16)
+
+
 def within(i, count):
     return lax.max(lax.min(i, count - 1), 0)
 
@@ -49,6 +85,18 @@
     return [
         xs[j] + ys[(j + 2 * k) % 4] + zs[j] + cs[k] for j in range(4) for k in range(2)
     ]
+
+
+def far_first(me, act):
+    x, y, z, c = coords(me)
+    xs = [lax.rem(x + j, 4) * 32 for j in range(4)]
+    ys = [lax.rem(y + j, 4) * 8 for j in range(4)]
+    zs = [lax.rem(z + j, 4) * 2 for j in range(4)]
+    cs = [c, 1 - c]
+    hops = (0, 1, 2, 1)
+    order = sorted(range(1, DEV), key=lambda k: -sum(hops[k >> s & 3] for s in (1, 3, 5)))
+    for k in order:
+        act(xs[k >> 5] + ys[k >> 3 & 3] + zs[k >> 1 & 3] + cs[k & 1])
 
 
 def for_all(me, act):
@@ -118,8 +166,9 @@
     mate_map,
     mate_coef,
     own_coarse,
-    coarse0,
-    coarse1,
+    packed0,
+    packed1,
+    table,
     planes_in,
     planes,
     cmaps,
@@ -142,11 +191,11 @@
     small_sem,
 ):
     me = lax.axis_index("leaf")
-    vals, recv, coarse = (vals0, vals1), (recv0, recv1), (coarse0, coarse1)
+    vals, recv, packed = (vals0, vals1), (recv0, recv1), (packed0, packed1)
     x, y, z, c = coords(me)
     line = x * 4 + y
     mate = me + 1 - 2 * c
-    is_server = (z == lax.rem(x + y, 4)) & (c == 1 - lax.rem(y, 2))
+    is_server = c == 1 - lax.rem(y, 2)
 
     barrier = pltpu.get_barrier_semaphore()
 
@@ -169,7 +218,7 @@
     ]
     for load in loads:
         load.start()
-    for_all(me, greet)
+    far_first(me, greet)
 
     coarse_rows = (
         (0, 4 * line, 4),
@@ -285,19 +334,16 @@
             ),
         )
 
-    def server_device(s):
-        sx, sy = lax.div(s, 4), lax.rem(s, 4)
-        sz = lax.rem(sx + sy, 4)
-        return (s * 4 + sz) * 2 + 1 - lax.rem(sy, 2)
-
-    def gather_copy(phase, i):
-        return remote(
-            own_coarse.at[phase],
-            coarse[phase].at[lax.div(me, 2)],
-            gather_send.at[phase],
-            gather_recv.at[phase],
-            server_device(2 * i + c),
-        )
+    def gather_copies(phase, i):
+        to_line = 2 * i + c
+        for v in range(4):
+            remote(
+                own_coarse.at[phase, v],
+                packed[phase].at[lax.div(me, 2)],
+                gather_send.at[phase],
+                gather_recv.at[phase],
+                (to_line * 4 + v) * 2 + 1 - c,
+            ).start()
 
     def mate_copy(phase):
         return remote(
@@ -343,9 +389,15 @@
         kids = jnp.concatenate(
             [jnp.where(c == 0, mine, theirs), jnp.where(c == 0, theirs, mine)], axis=0
         ).astype(jnp.bfloat16)
-        own_coarse[phase] = mm(maps_t[15], kids).astype(jnp.bfloat16)
-        for i in range(8):
-            gather_copy(phase, i).start()
+        made = mm(maps_t[15], kids)
+        for v in range(4):
+            own_coarse[phase, v] = pack(made, -v)
+
+        def spread(i, carry):
+            gather_copies(phase, i)
+            return carry
+
+        lax.fori_loop(0, 8, spread, 0)
 
     def fill(lo, hi):
         def one(d, carry):
@@ -393,8 +445,13 @@
         lax.fori_loop(0, 62, turn_coarse, 0, unroll=2)
 
     def serve(phase):
-        table = coarse[phase]
-        take(table.at[pl.ds(0, 64)], gather_recv.at[phase])
+        take(packed[phase], gather_recv.at[phase])
+
+        def open_up(n, carry):
+            table[n] = unpack(packed[phase], n)
+            return carry
+
+        lax.fori_loop(0, 64, open_up, 0, unroll=8)
         for level in range(5):
             at, above = COARSE_AT[level], COARSE_AT[level + 1]
 
@@ -430,19 +487,18 @@
             g = (terms[4 + i] + mm(cmaps[rows[1] + i], f)).astype(jnp.bfloat16)
             for j in range(2):
                 n = 2 * i + j
-                f1_out[phase, n] = (
-                    terms[n] + mm(cmaps[rows[0] + n], g)
-                ).astype(jnp.bfloat16)
+                whole = terms[n] + mm(cmaps[rows[0] + n], g)
+                f1_out[phase, n] = pack(whole, 0)
         for o in range(1, 8):
             f1_copy(phase, o).start()
-        f1_in[phase] = f1_out[phase, z]
+        f1_in[phase, z] = f1_out[phase, z]
 
     def f1_copy(phase, o):
         tz = lax.rem(z + o // 2, 4)
         to = (line * 4 + tz) * 2 + lax.rem(c + o % 2, 2)
         return remote(
             f1_out.at[phase, tz],
-            f1_in.at[phase],
+            f1_in.at[phase, z],
             f1_send.at[phase],
             f1_recv.at[phase],
             to,
@@ -453,14 +509,15 @@
             lax.fori_loop(0, LEAVES, turn_basis, 0, unroll=4)
             lax.fori_loop(0, LEAVES * LEAF // COLS, mark, 0, unroll=4)
 
-        @pl.when(is_server)
-        def _():
-            serve(phase)
+        if phase == 0:
+            loads[4].wait()
+
+            @pl.when(is_server)
+            def _():
+                serve(phase)
 
         for h in halo_copies(phase):
             h.wait_recv()
-        if phase == 0:
-            loads[4].wait()
 
         def pair(t, carry):
             near_leaf(phase, 2 * t)
@@ -468,6 +525,11 @@
             return carry
 
         lax.fori_loop(0, LEAVES // 2, pair, 0)
+        if phase == 1:
+
+            @pl.when(is_server)
+            def _():
+                serve(phase)
 
     def finish(phase):
         if phase == 0:
@@ -497,8 +559,12 @@
         def _():
             take(f1_in.at[phase], f1_recv.at[phase])
 
+        @pl.when(is_server)
+        def _():
+            take(f1_in.at[phase, pl.ds(0, 3)], f1_recv.at[phase])
+
         field[NODES - 1] = (
-            coupled[NODES - 1] + mm(maps[NODES - 1], f1_in[phase])
+            coupled[NODES - 1] + mm(maps[NODES - 1], join(f1_in, phase))
         ).astype(jnp.bfloat16)
         for height in range(3, -1, -1):
             for j in range(LEAVES >> (height + 1)):
@@ -534,7 +600,7 @@
     map_copy.start()
     mate_copy(0).start()
 
-    for_all(me, list_copy)
+    far_first(me, list_copy)
 
     @pl.when(is_server)
     def _():
@@ -542,9 +608,9 @@
 
     take(requests.at[pl.ds(0, DEV - 1)], list_sem.at[1])
     mine = (lax.broadcasted_iota(jnp.int32, (8, DEV), 1) == me).astype(jnp.bfloat16)
-    table = requests[...].reshape(DEV, COLS).astype(jnp.float32).astype(jnp.bfloat16)
+    asks = requests[...].reshape(DEV, COLS).astype(jnp.float32).astype(jnp.bfloat16)
     wanted = lax.dot_general(
-        mine, table, (((1,), (1,)), ((), ())), preferred_element_type=jnp.float32
+        mine, asks, (((1,), (1,)), ((), ())), preferred_element_type=jnp.float32
     )
     chosen_v[...] = jnp.clip(wanted, 0, NODES - 1).astype(jnp.int32)
     small = pltpu.make_async_copy(chosen_v, chosen, small_sem)
@@ -582,11 +648,11 @@
     for phase in range(2):
         for h in halo_copies(phase):
             h.wait_send()
-        take(coarse[phase].at[pl.ds(0, 8)], gather_send.at[phase])
+        take(packed[phase].at[pl.ds(0, 32)], gather_send.at[phase])
 
         @pl.when(is_server)
         def _():
-            take(coarse[phase].at[pl.ds(0, 7)], f1_send.at[phase])
+            take(packed[phase].at[pl.ds(0, 7)], f1_send.at[phase])
 
 
 def local(
@@ -633,16 +699,17 @@
         pltpu.SMEM((8, DEV), i32),
         pltpu.VMEM((RANK, RANK), bf16),
         pltpu.VMEM((2, RANK, COLS), bf16),
-        pltpu.VMEM((2, RANK, COLS), bf16),
-        pltpu.VMEM((COARSE, RANK, COLS), bf16),
+        pltpu.VMEM((2, 4, 16, COLS), bf16),
+        pltpu.VMEM((64, 16, COLS), bf16),
+        pltpu.VMEM((64, 16, COLS), bf16),
         pltpu.VMEM((COARSE, RANK, COLS), bf16),
         pltpu.VMEM((RANK, RANK, COARSE - 2), bf16),
         pltpu.VMEM(((RANK + 1) * (COARSE - 2), RANK), f32),
         pltpu.VMEM((COARSE - 2, RANK, RANK), bf16),
         pltpu.VMEM((62, RANK, 2 * RANK), bf16),
         pltpu.VMEM((10, RANK, 4 * RANK), bf16),
-        pltpu.VMEM((2, 4, RANK, COLS), bf16),
-        pltpu.VMEM((2, RANK, COLS), bf16),
+        pltpu.VMEM((2, 4, 16, COLS), bf16),
+        pltpu.VMEM((2, 4, 16, COLS), bf16),
         dma((5,)),
         dma((7,)),
         dma((2,)),

time: 94.8 us -> 86.7 us (0.915); the launches traced: 93.3 us -> 86.5 us
  Pallas kernels: 90 us -> 83.2 us
    pallas_call x1, Pallas kernels: 90 us -> 83.2 us  [local(): pl.pallas_call(kernel, out_shape=(pltpu.VMEM((points, COLS), f32), pltpu....]
where the time goes in v2:
time: 86.7 us; the launch traced here: 86.5 us
  Pallas kernels  83.2 us (96%)
  local copies, waits for them, and re-layouts  2.64 us (3%)
    pallas_call x1, Pallas kernels, local(): pl.pallas_call(kernel, out_shape=(pltpu.VMEM((points, COLS), f32), pltpu....  83.2 us
    unnamed x2, local copies, waits for them, and re-layouts  2.64 us

profile of v2, /device:TPU:1, one launch (start us, length us, event | category | flops | bytes accessed | tf_op | source)
XLA Modules:
  0.0 86.5 jit_solution(9189796244500462421)
XLA Ops:
  0.6 83.2 %shard_map.122 = (f32[4096,128]{1,0:T(8,128)S(1)}, f32[4096,128]{1,0:T(8,128)S(1)}) custom-call(s32[4,31]{1,0:T(4,128)} %bitcast.7, s32[2,16]{1,0:T(2,128)} %bitcast.10, s32[4,126]{1,0:T(4,128)} %bitcast.9, s32[4,31]{1,0:T(4,128)} %bitcast.8, s32[32,128]{1,0:T(8,128)} %bitcast.6, f32[4096,128]{1,0:T(8,128)} %weights_h.1, bf16[16,64,256]{2,1,0:T(8,128)(2,1)} %basis_h.1, ...), custom_call_target="tpu_custom_call" | custom-call | tf_op jit(solution)/shard_map/pallas_call | solution.py:727
  83.8 1.3 %copy.15 = f32[4096,128]{1,0:T(8,128)} copy(f32[4096,128]{1,0:T(8,128)S(1)} %get-tuple-element.2) | data formatting | bytes 4194304
  85.2 1.3 %copy.16 = f32[4096,128]{1,0:T(8,128)} copy(f32[4096,128]{1,0:T(8,128)S(1)} %get-tuple-element.3) | data formatting | bytes 4194304

commit v3 on v2

--- a/solution.py
+++ b/solution.py
@@ -99,16 +99,18 @@
         act(xs[k >> 5] + ys[k >> 3 & 3] + zs[k >> 1 & 3] + cs[k & 1])
 
 
-def for_all(me, act):
-    for device in batch_of(me, 0)[1:]:
-        act(device)
+def for_some(me, act, lo, hi):
+    if lo == 0:
+        for device in batch_of(me, 0)[1:]:
+            act(device)
+        lo = 1
 
     def one(b, carry):
         for device in batch_of(me, b):
             act(device)
         return carry
 
-    lax.fori_loop(1, BATCHES, one, 0)
+    lax.fori_loop(lo, hi, one, 0)
 
 
 def remote(src, dst, send_sem, recv_sem, device):
@@ -127,11 +129,10 @@
 
 
 def kernel(
-    sources_s,
-    near_ids_s,
-    coarse_sources_s,
-    sources_v,
-    labels_v,
+    sources_h,
+    near_ids_h,
+    coarse_sources_h,
+    labels_h,
     weights_h,
     basis_h,
     near_h,
@@ -139,22 +140,25 @@
     couplings_h,
     coarse_transfer_h,
     coarse_couplings_h,
-    updated,
-    scores,
+    based,
+    acc,
+    field,
+    basis_t,
+    sources_s,
+    near_ids_s,
+    coarse_sources_s,
+    sources_v,
+    labels_v,
     w,
-    based,
     shift,
     vals0,
     vals1,
-    acc,
     near,
     basis,
-    basis_t,
     maps,
     maps_t,
     blocks,
     coef,
-    field,
     coupled,
     send,
     recv0,
@@ -208,10 +212,15 @@
         pltpu.make_async_copy(src, dst, in_sem.at[i])
         for i, (src, dst) in enumerate(
             (
+                (sources_h, sources_v),
                 (weights_h, w),
                 (basis_h, basis),
                 (transfer_h, maps),
                 (couplings_h, blocks),
+                (sources_h, sources_s),
+                (near_ids_h, near_ids_s),
+                (coarse_sources_h, coarse_sources_s),
+                (labels_h, labels_v),
                 (near_h, near),
             )
         )
@@ -250,6 +259,7 @@
     for height in range(1, 5):
         bits = jnp.where(node >= STARTS[height], 4 - height, bits)
         first = jnp.where(node >= STARTS[height], STARTS[height], first)
+    loads[0].wait()
     name = sources_v[...]
     owner = lax.shift_right_logical(name, bits)
     row = first + name - lax.shift_left(owner, bits)
@@ -284,10 +294,10 @@
                 kids = coef[lo : lo + 2].reshape(2 * RANK, COLS)
                 coef[up] = mm(maps_t[up - LEAVES], kids).astype(jnp.bfloat16)
 
-    loads[0].wait()
     loads[1].wait()
+    loads[2].wait()
     lax.fori_loop(0, LEAVES, half_round, 0, unroll=4)
-    loads[2].wait()
+    loads[3].wait()
 
     def turn(j, carry):
         lo = 2 * j
@@ -311,6 +321,8 @@
         shift[rows, :] = jnp.where(column == lane, 0.25, -0.25).astype(jnp.bfloat16)
         return carry
 
+    for load in loads[4:9]:
+        load.wait()
     pl.semaphore_wait(barrier, DEV - 1)
 
     def halo_copies(phase):
@@ -416,8 +428,8 @@
         total += mm(near[t, 2], vals[phase][b])
         acc[rows, :] = total
 
-    def send_blocks(phase):
-        for_all(me, lambda device: block_copy(phase, device))
+    def send_blocks(phase, lo, hi):
+        for_some(me, lambda device: block_copy(phase, device), lo, hi)
 
     def blocks_sent(phase):
         take(send.at[pl.ds(0, DEV - 1)], block_send.at[phase])
@@ -510,7 +522,7 @@
             lax.fori_loop(0, LEAVES * LEAF // COLS, mark, 0, unroll=4)
 
         if phase == 0:
-            loads[4].wait()
+            loads[9].wait()
 
             @pl.when(is_server)
             def _():
@@ -532,8 +544,6 @@
                 serve(phase)
 
     def finish(phase):
-        if phase == 0:
-            loads[3].wait()
         take(recv[phase].at[pl.ds(0, DEV - 1)], block_recv.at[phase])
 
         def couple(t, bits):
@@ -588,13 +598,6 @@
 
     def second_coef(t, carry):
         coef[t] = mm(basis[t], vals1[t + HALO]).astype(jnp.bfloat16)
-        return carry
-
-    def last_leaf(t, carry):
-        rows = pl.ds(pl.multiple_of(t * LEAF, LEAF), LEAF)
-        score = acc[rows, :] + mm(basis_t[t], field[t])
-        scores[rows, :] = score
-        updated[rows, :] = based[rows, :] - 0.25 * jnp.tanh(0.5 * score)
         return carry
 
     map_copy.start()
@@ -621,7 +624,7 @@
     small.wait()
     fill(0, DEV)
     recv0[me] = coef[within(chosen[0, me], NODES)]
-    send_blocks(0)
+    send_blocks(0, 0, BATCHES)
     exchange(0)
     finish(0)
     lax.fori_loop(0, LEAVES, first_leaf, 0, unroll=4)
@@ -635,11 +638,11 @@
     mate_copy(1).start()
     fill(0, DEV)
     recv1[me] = coef[within(chosen[0, me], NODES)]
+    send_blocks(1, 0, 2)
     send_top(1)
-    send_blocks(1)
+    send_blocks(1, 2, BATCHES)
     exchange(1)
     finish(1)
-    lax.fori_loop(0, LEAVES, last_leaf, 0, unroll=4)
 
     map_copy.wait_send()
     take(requests.at[pl.ds(0, DEV - 1)], list_sem.at[0])
@@ -653,6 +656,24 @@
         @pl.when(is_server)
         def _():
             take(packed[phase].at[pl.ds(0, 7)], f1_send.at[phase])
+
+
+def last_kernel(based, near_term, field, basis_t, updated_h, scores_h, updated, scores, sem):
+    copies = []
+    for part in range(4):
+        for t in range(4 * part, 4 * part + 4):
+            rows = pl.ds(t * LEAF, LEAF)
+            score = near_term[rows, :] + mm(basis_t[t], field[t])
+            scores[rows, :] = score
+            updated[rows, :] = based[rows, :] - 0.25 * jnp.tanh(0.5 * score)
+        rows = pl.ds(4 * part * LEAF, 4 * LEAF)
+        for i, (src, dst) in enumerate(((updated, updated_h), (scores, scores_h))):
+            copies.append(
+                pltpu.make_async_copy(src.at[rows], dst.at[rows], sem.at[i, part])
+            )
+            copies[-1].start()
+    for copy in copies:
+        copy.wait()
 
 
 def local(
@@ -670,24 +691,24 @@
 ):
     bf16, f32, i32 = jnp.bfloat16, jnp.float32, jnp.int32
     points = LEAVES * LEAF
-    smem = pl.BlockSpec(memory_space=pltpu.SMEM)
     vmem = pl.BlockSpec(memory_space=pltpu.VMEM)
     hbm = pl.BlockSpec(memory_space=pl.ANY)
     dma = pltpu.SemaphoreType.DMA
     scratch = [
-        pltpu.VMEM((points, COLS), f32),
+        pltpu.SMEM((4, NODES), i32),
+        pltpu.SMEM((2, LEAVES), i32),
+        pltpu.SMEM((4, COARSE), i32),
+        pltpu.VMEM((4, NODES), i32),
+        pltpu.VMEM((points // COLS, COLS), i32),
         pltpu.VMEM((points, COLS), f32),
         pltpu.VMEM((points, COLS), bf16),
         pltpu.VMEM((LEAVES + 2 * HALO, LEAF, COLS), bf16),
         pltpu.VMEM((LEAVES + 2 * HALO, LEAF, COLS), bf16),
-        pltpu.VMEM((points, COLS), f32),
         pltpu.VMEM((LEAVES, 3, LEAF, LEAF), bf16),
         pltpu.VMEM((LEAVES, RANK, LEAF), bf16),
-        pltpu.VMEM((LEAVES, LEAF, RANK), bf16),
         pltpu.VMEM((NODES, RANK, RANK), bf16),
         pltpu.VMEM((16, RANK, 2 * RANK), bf16),
         pltpu.VMEM((NODES, RANK, 4 * RANK), bf16),
-        pltpu.VMEM((NODES, RANK, COLS), bf16),
         pltpu.VMEM((NODES, RANK, COLS), bf16),
         pltpu.VMEM((NODES, RANK, COLS), f32),
         pltpu.VMEM((DEV, RANK, COLS), bf16),
@@ -710,7 +731,7 @@
         pltpu.VMEM((10, RANK, 4 * RANK), bf16),
         pltpu.VMEM((2, 4, 16, COLS), bf16),
         pltpu.VMEM((2, 4, 16, COLS), bf16),
-        dma((5,)),
+        dma((10,)),
         dma((7,)),
         dma((2,)),
         dma((2, 2)),
@@ -724,14 +745,16 @@
         dma((2,)),
         dma(()),
     ]
-    return pl.pallas_call(
+    parts = pl.pallas_call(
         kernel,
         out_shape=(
             pltpu.VMEM((points, COLS), f32),
             pltpu.VMEM((points, COLS), f32),
+            pltpu.VMEM((NODES, RANK, COLS), bf16),
+            pltpu.VMEM((LEAVES, LEAF, RANK), bf16),
         ),
-        in_specs=[smem, smem, smem, vmem, vmem] + [hbm] * 7,
-        out_specs=(vmem, vmem),
+        in_specs=[hbm] * 11,
+        out_specs=(vmem, vmem, vmem, vmem),
         scratch_shapes=scratch,
         compiler_params=pltpu.CompilerParams(
             collective_id=0, has_side_effects=True, vmem_limit_bytes=58 << 20
@@ -740,7 +763,6 @@
         sources.T,
         near_ids.T,
         coarse_sources.T,
-        sources.T,
         labels.reshape(points // COLS, COLS),
         weights,
         basis,
@@ -750,6 +772,21 @@
         coarse_transfer.transpose(1, 2, 0),
         coarse_couplings,
     )
+    return pl.pallas_call(
+        last_kernel,
+        out_shape=(
+            jax.ShapeDtypeStruct((points, COLS), f32),
+            jax.ShapeDtypeStruct((points, COLS), f32),
+        ),
+        in_specs=[vmem] * 4,
+        out_specs=(hbm, hbm),
+        scratch_shapes=[
+            pltpu.VMEM((points, COLS), f32),
+            pltpu.VMEM((points, COLS), f32),
+            dma((2, 4)),
+        ],
+        compiler_params=pltpu.CompilerParams(vmem_limit_bytes=16 << 20),
+    )(*parts)
 
 
 def solution(mesh):

time: 86.7 us -> 84.7 us (0.977)
  local copies, waits for them, and re-layouts: 2.64 us -> 0 us
    unnamed x2 -> x0, local copies, waits for them, and re-layouts: 2.64 us -> none
    pallas_call x0 -> x1, Pallas kernels: none -> 2.31 us  [local(): pl.pallas_call(last_kernel, out_shape=(jax.ShapeDtypeStruct((points, COLS...]
    pallas_call x1, Pallas kernels: 83.2 us -> 80.9 us  [local(): pl.pallas_call(kernel, out_shape=(pltpu.VMEM((points, COLS), f32), pltpu....]
where the time goes in v3:
time: 84.7 us; the launch traced here: 83.9 us
  Pallas kernels  83.2 us (98%)
    pallas_call x1, Pallas kernels, local(): pl.pallas_call(kernel, out_shape=(pltpu.VMEM((points, COLS), f32), pltpu....  80.9 us
    pallas_call x1, Pallas kernels, local(): pl.pallas_call(last_kernel, out_shape=(jax.ShapeDtypeStruct((points, COLS...  2.31 us

profile of v3, /device:TPU:1, one launch (start us, length us, event | category | flops | bytes accessed | tf_op | source)
XLA Modules:
  0.0 83.9 jit_solution(16879881684026061917)
XLA Ops:
  0.6 80.9 %shard_map.122 = (f32[4096,128]{1,0:T(8,128)S(1)}, f32[4096,128]{1,0:T(8,128)S(1)}, bf16[31,64,128]{2,1,0:T(8,128)(2,1)S(1)}, bf16[16,256,64]{2,1,0:T(8,128)(2,1)S(1)}) custom-call(s32[4,31]{1,0:T(4,128)} %bitcast.7, s32[2,16]{1,0:T(2,128)} %bitcast.9, s32[4,126]{1,0:T(4,128)} %bitcast.8, s32[32,128]{1,0:T(8,128)} %bitcast.6, f32[4096,128]{1,0:T(8,128)} %weights_h.1, ...), custom_call_target="tpu_custom_call" | custom-call | tf_op jit(solution)/shard_map/pallas_call | solution.py:748
  81.6 2.3 %shard_map.123 = (f32[4096,128]{1,0:T(8,128)}, f32[4096,128]{1,0:T(8,128)}) custom-call(f32[4096,128]{1,0:T(8,128)S(1)} %get-tuple-element.6.based, f32[4096,128]{1,0:T(8,128)S(1)} %get-tuple-element.7.near_term, bf16[31,64,128]{2,1,0:T(8,128)(2,1)S(1)} %get-tuple-element.8.field, bf16[16,256,64]{2,1,0:T(8,128)(2,1)S(1)} %get-tuple-element.9.basis_t), custom_call_target="tpu_custom_call" | custom-call | tf_op jit(solution)/shard_map/pallas_call | solution.py:775

commit v4 on v3

--- a/solution.py
+++ b/solution.py
@@ -153,6 +153,8 @@
     shift,
     vals0,
     vals1,
+    halo0,
+    halo1,
     near,
     basis,
     maps,
@@ -196,6 +198,7 @@
 ):
     me = lax.axis_index("leaf")
     vals, recv, packed = (vals0, vals1), (recv0, recv1), (packed0, packed1)
+    halo = (halo0, halo1)
     x, y, z, c = coords(me)
     line = x * 4 + y
     mate = me + 1 - 2 * c
@@ -282,7 +285,7 @@
     def half_round(t, carry):
         rows = pl.ds(pl.multiple_of(t * LEAF, LEAF), LEAF)
         v = w[rows, :].astype(jnp.bfloat16)
-        vals0[t + HALO] = v
+        vals0[t] = v
         coef[t] = mm(basis[t], v).astype(jnp.bfloat16)
         return carry
 
@@ -331,15 +334,15 @@
         v = vals[phase]
         return (
             remote(
-                v.at[pl.ds(LEAVES, HALO)],
-                v.at[pl.ds(0, HALO)],
+                v.at[pl.ds(LEAVES - HALO, HALO)],
+                halo[phase].at[pl.ds(0, HALO)],
                 halo_send.at[phase, 0],
                 halo_recv.at[phase, 0],
                 after,
             ),
             remote(
-                v.at[pl.ds(HALO, HALO)],
-                v.at[pl.ds(LEAVES + HALO, HALO)],
+                v.at[pl.ds(0, HALO)],
+                halo[phase].at[pl.ds(HALO, HALO)],
                 halo_send.at[phase, 1],
                 halo_recv.at[phase, 1],
                 before,
@@ -418,14 +421,18 @@
 
         lax.fori_loop(lo, hi, one, 0, unroll=8)
 
-    def near_leaf(phase, t):
-        base = me * LEAVES - HALO
-        a = within(near_ids_s[0, t] - base, LEAVES + 2 * HALO)
-        b = within(near_ids_s[1, t] - base, LEAVES + 2 * HALO)
+    def near_leaf(phase, t, edge):
         rows = pl.ds(pl.multiple_of(t * LEAF, LEAF), LEAF)
-        total = mm(near[t, 0], vals[phase][t + HALO])
-        total += mm(near[t, 1], vals[phase][a])
-        total += mm(near[t, 2], vals[phase][b])
+        total = mm(near[t, 0], vals[phase][t])
+        for i in range(2):
+            at = near_ids_s[i, t] - me * LEAVES
+            v = vals[phase][within(at, LEAVES)]
+            if edge:
+                inside = (at >= 0) & (at < LEAVES)
+                slot = jnp.where(at < 0, at + HALO, at + HALO - LEAVES)
+                far = halo[phase][within(slot, 2 * HALO)]
+                v = jnp.where(inside, v, far)
+            total += mm(near[t, i + 1], v)
         acc[rows, :] = total
 
     def send_blocks(phase, lo, hi):
@@ -528,15 +535,22 @@
             def _():
                 serve(phase)
 
+
+        def pair(t, carry):
+            near_leaf(phase, 2 * t, False)
+            near_leaf(phase, 2 * t + 1, False)
+            return carry
+
+        lax.fori_loop(1, LEAVES // 2 - 1, pair, 0)
         for h in halo_copies(phase):
             h.wait_recv()
 
-        def pair(t, carry):
-            near_leaf(phase, 2 * t)
-            near_leaf(phase, 2 * t + 1)
+        def edge_pair(i, carry):
+            near_leaf(phase, i * (LEAVES - HALO), True)
+            near_leaf(phase, i * (LEAVES - HALO) + 1, True)
             return carry
 
-        lax.fori_loop(0, LEAVES // 2, pair, 0)
+        lax.fori_loop(0, 2, edge_pair, 0)
         if phase == 1:
 
             @pl.when(is_server)
@@ -593,11 +607,11 @@
         middle = w[rows, :] + (marked - 0.25 * jnp.tanh(0.5 * score))
         based[rows, :] = middle + marked
         v = middle.astype(jnp.bfloat16)
-        vals1[t + HALO] = v
+        vals1[t] = v
         return carry
 
     def second_coef(t, carry):
-        coef[t] = mm(basis[t], vals1[t + HALO]).astype(jnp.bfloat16)
+        coef[t] = mm(basis[t], vals1[t]).astype(jnp.bfloat16)
         return carry
 
     map_copy.start()
@@ -619,12 +633,13 @@
     small = pltpu.make_async_copy(chosen_v, chosen, small_sem)
     small.start()
     send_top(0)
-    for h in halo_copies(0):
-        h.start()
     small.wait()
     fill(0, DEV)
     recv0[me] = coef[within(chosen[0, me], NODES)]
-    send_blocks(0, 0, BATCHES)
+    send_blocks(0, 0, 8)
+    for h in halo_copies(0):
+        h.start()
+    send_blocks(0, 8, BATCHES)
     exchange(0)
     finish(0)
     lax.fori_loop(0, LEAVES, first_leaf, 0, unroll=4)
@@ -702,8 +717,10 @@
         pltpu.VMEM((points // COLS, COLS), i32),
         pltpu.VMEM((points, COLS), f32),
         pltpu.VMEM((points, COLS), bf16),
-        pltpu.VMEM((LEAVES + 2 * HALO, LEAF, COLS), bf16),
-        pltpu.VMEM((LEAVES + 2 * HALO, LEAF, COLS), bf16),
+        pltpu.VMEM((LEAVES, LEAF, COLS), bf16),
+        pltpu.VMEM((LEAVES, LEAF, COLS), bf16),
+        pltpu.VMEM((2 * HALO, LEAF, COLS), bf16),
+        pltpu.VMEM((2 * HALO, LEAF, COLS), bf16),
         pltpu.VMEM((LEAVES, 3, LEAF, LEAF), bf16),
         pltpu.VMEM((LEAVES, RANK, LEAF), bf16),
         pltpu.VMEM((NODES, RANK, RANK), bf16),

time: 84.7 us -> 83.9 us (level)
  no operation moved by 1% of the time
where the time goes in v4:
time: 83.9 us; the launch traced here: 83.8 us
  Pallas kernels  83.2 us (99%)
    pallas_call x1, Pallas kernels, local(): pl.pallas_call(kernel, out_shape=(pltpu.VMEM((points, COLS), f32), pltpu....  80.9 us
    pallas_call x1, Pallas kernels, local(): pl.pallas_call(last_kernel, out_shape=(jax.ShapeDtypeStruct((points, COLS...  2.3 us

profile of v4, /device:TPU:1, one launch (start us, length us, event | category | flops | bytes accessed | tf_op | source)
XLA Modules:
  0.0 83.8 jit_solution(811204802335225084)
XLA Ops:
  0.6 80.9 %shard_map.122 = (f32[4096,128]{1,0:T(8,128)S(1)}, f32[4096,128]{1,0:T(8,128)S(1)}, bf16[31,64,128]{2,1,0:T(8,128)(2,1)S(1)}, bf16[16,256,64]{2,1,0:T(8,128)(2,1)S(1)}) custom-call(s32[4,31]{1,0:T(4,128)} %bitcast.7, s32[2,16]{1,0:T(2,128)} %bitcast.9, s32[4,126]{1,0:T(4,128)} %bitcast.8, s32[32,128]{1,0:T(8,128)} %bitcast.6, f32[4096,128]{1,0:T(8,128)} %weights_h.1, ...), custom_call_target="tpu_custom_call" | custom-call | tf_op jit(solution)/shard_map/pallas_call | solution.py:765
  81.5 2.3 %shard_map.123 = (f32[4096,128]{1,0:T(8,128)}, f32[4096,128]{1,0:T(8,128)}) custom-call(f32[4096,128]{1,0:T(8,128)S(1)} %get-tuple-element.6.based, f32[4096,128]{1,0:T(8,128)S(1)} %get-tuple-element.7.near_term, bf16[31,64,128]{2,1,0:T(8,128)(2,1)S(1)} %get-tuple-element.8.field, bf16[16,256,64]{2,1,0:T(8,128)(2,1)S(1)} %get-tuple-element.9.basis_t), custom_call_target="tpu_custom_call" | custom-call | tf_op jit(solution)/shard_map/pallas_call | solution.py:792

commit v5 on v4

--- a/solution.py
+++ b/solution.py
@@ -415,11 +415,10 @@
         lax.fori_loop(0, 8, spread, 0)
 
     def fill(lo, hi):
-        def one(d, carry):
-            send[d] = coef[within(chosen[0, d], NODES)]
-            return carry
-
-        lax.fori_loop(lo, hi, one, 0, unroll=8)
+        def one(device):
+            send[device] = coef[within(chosen[0, device], NODES)]
+
+        for_some(me, one, lo, hi)
 
     def near_leaf(phase, t, edge):
         rows = pl.ds(pl.multiple_of(t * LEAF, LEAF), LEAF)
@@ -634,9 +633,11 @@
     small.start()
     send_top(0)
     small.wait()
-    fill(0, DEV)
+    fill(0, 2)
+    send_blocks(0, 0, 2)
+    fill(2, BATCHES)
     recv0[me] = coef[within(chosen[0, me], NODES)]
-    send_blocks(0, 0, 8)
+    send_blocks(0, 2, 8)
     for h in halo_copies(0):
         h.start()
     send_blocks(0, 8, BATCHES)
@@ -651,9 +652,10 @@
     mate_copy(0).wait_send()
     climb()
     mate_copy(1).start()
-    fill(0, DEV)
+    fill(0, 2)
+    send_blocks(1, 0, 2)
+    fill(2, BATCHES)
     recv1[me] = coef[within(chosen[0, me], NODES)]
-    send_blocks(1, 0, 2)
     send_top(1)
     send_blocks(1, 2, BATCHES)
     exchange(1)

time: 83.9 us -> 84 us (level)
  no operation moved by 1% of the time
where the time goes in v5:
time: 84 us; the launch traced here: 83.9 us
  Pallas kernels  83.2 us (99%)
    pallas_call x1, Pallas kernels, local(): pl.pallas_call(kernel, out_shape=(pltpu.VMEM((points, COLS), f32), pltpu....  80.9 us
    pallas_call x1, Pallas kernels, local(): pl.pallas_call(last_kernel, out_shape=(jax.ShapeDtypeStruct((points, COLS...  2.31 us

profile of v5, /device:TPU:1, one launch (start us, length us, event | category | flops | bytes accessed | tf_op | source)
XLA Modules:
  0.0 83.9 jit_solution(1062079023451077935)
XLA Ops:
  0.6 80.9 %shard_map.122 = (f32[4096,128]{1,0:T(8,128)S(1)}, f32[4096,128]{1,0:T(8,128)S(1)}, bf16[31,64,128]{2,1,0:T(8,128)(2,1)S(1)}, bf16[16,256,64]{2,1,0:T(8,128)(2,1)S(1)}) custom-call(s32[4,31]{1,0:T(4,128)} %bitcast.7, s32[2,16]{1,0:T(2,128)} %bitcast.9, s32[4,126]{1,0:T(4,128)} %bitcast.8, s32[32,128]{1,0:T(8,128)} %bitcast.6, f32[4096,128]{1,0:T(8,128)} %weights_h.1, ...), custom_call_target="tpu_custom_call" | custom-call | tf_op jit(solution)/shard_map/pallas_call | solution.py:767
  81.5 2.3 %shard_map.123 = (f32[4096,128]{1,0:T(8,128)}, f32[4096,128]{1,0:T(8,128)}) custom-call(f32[4096,128]{1,0:T(8,128)S(1)} %get-tuple-element.6.based, f32[4096,128]{1,0:T(8,128)S(1)} %get-tuple-element.7.near_term, bf16[31,64,128]{2,1,0:T(8,128)(2,1)S(1)} %get-tuple-element.8.field, bf16[16,256,64]{2,1,0:T(8,128)(2,1)S(1)} %get-tuple-element.9.basis_t), custom_call_target="tpu_custom_call" | custom-call | tf_op jit(solution)/shard_map/pallas_call | solution.py:794
